TPU v7x, 32 devices: a whole 2x2x4 slice. The times are simulated.
32 devices in a mesh: dom: 8 (over z, y), group: 4 (over x, core).
Axes of the slice: x: 2, y: 2, z: 4, core: 2. Of those that a mesh axis runs over, the one named last changes fastest.
Arguments:
- features: bfloat16 [4096, 1024], P(('dom', 'group')), may hold values from -6 to 6
- out_grad: bfloat16 [4096, 1024], P(('dom', 'group')), may hold values from -0.1796875 to 0.1796875
- gcn_weight: bfloat16 [1024, 1024], replicated, may hold values from -0.1875 to 0.1875
- tile_index: int32 [32, 4], P(('dom', 'group')), may hold values from 0 to 2
- tile_edges: int32 [32, 4, 128, 128], P(('dom', 'group')), may hold values 0 or 1
- halo_rows: int32 [8, 4, 8, 32], P('dom', 'group'), may hold values from 0 to 127
- routes: int32 [4096, 2], P(('dom', 'group')), may hold values from 0 to 15, all different within a row; in each aligned block of 128 rows (0 to 127, 128 to 255, ...) at most 20 rows name the same one
- route_weight: float32 [4096, 2], P(('dom', 'group')), may hold values from 0.25 to 1
- up_weight: bfloat16 [16, 1024, 4096], P('dom', None, 'group'), may hold values from -0.1875 to 0.1875
- down_weight: bfloat16 [16, 4096, 1024], P('dom', 'group'), may hold values from -0.09375 to 0.09375
Outputs:
- node_out: bfloat16 [4096, 1024], P(('dom', 'group'))
- up_grad: bfloat16 [16, 1024, 4096], P('dom', None, 'group')
- down_grad: bfloat16 [16, 4096, 1024], P('dom', 'group')
Inputs may be any that keep to these rules, and one draw needn't show every extreme that they name: `routes`: in the rows of one partition no expert is named more than 20 times, and in every draw some partition names some expert exactly 20 times.
All inputs are finite; a program needn't handle non-finite values. No bound on the sum of `tile_edges` on one device may be relied on, other than what follows from the above.
Results may differ from a plain program's by a relative error of at most 0.0071.
Values may be sent and summed in bfloat16 or wider, within the bound.
A program may use at most 128 MiB of HBM per device.

v0:
```python
import jax
import jax.numpy as jnp
from jax import lax
from jax.sharding import PartitionSpec as P


def silu_slope(values):
    logistic = jax.nn.sigmoid(values)
    return logistic * (1.0 + values * (1.0 - logistic))


def slot_table(route_rows, expert_count, capacity):
    flat_ids = route_rows.reshape(-1)
    onehot = (flat_ids[:, None] == jnp.arange(expert_count, dtype=jnp.int32)[None, :]).astype(
        jnp.int32
    )
    before = jnp.cumsum(onehot, axis=0) - onehot
    within = jnp.sum(before * onehot, axis=1)
    target = flat_ids * capacity + within
    filler = (
        jnp.zeros((expert_count * capacity,), jnp.int32)
        .at[target]
        .set(jnp.arange(flat_ids.shape[0], dtype=jnp.int32) + 1)
    )
    return (target, filler)


def local(
    features,
    out_grad,
    gcn_weight,
    tile_index,
    tile_edges,
    halo_rows,
    routes,
    route_weight,
    up_weight,
    down_weight,
):
    dom_count = lax.axis_size("dom")
    group_count = lax.axis_size("group")
    node_count, width = features.shape
    tile_rows = tile_edges.shape[-1]
    local_tiles = tile_index.shape[0]
    border_rows = halo_rows.shape[-1]
    expert_local = up_weight.shape[0]
    expert_count = expert_local * dom_count
    top_count = routes.shape[1]
    capacity = max(2, 5 * node_count * top_count // (4 * expert_count))
    send_lists = halo_rows.reshape(-1)
    outgoing = features[send_lists].reshape(dom_count, border_rows, width)
    incoming = lax.all_to_all(outgoing, "dom", split_axis=0, concat_axis=0, tiled=True)
    sources = jnp.concatenate(
        [features, incoming.reshape(dom_count * border_rows, width)], axis=0
    ).reshape(-1, tile_rows, width)
    chosen = sources[tile_index]
    edge_values = tile_edges.astype(jnp.bfloat16)
    summed = features.reshape(local_tiles, tile_rows, width).astype(jnp.float32) + jnp.einsum(
        "tsij,tsjd->tid", edge_values, chosen, preferred_element_type=jnp.float32
    )
    degree = 1.0 + jnp.sum(tile_edges, axis=(1, 3)).astype(jnp.float32)
    aggregated = (
        (summed / jnp.sqrt(degree)[:, :, None]).reshape(node_count, width).astype(jnp.bfloat16)
    )
    preact = jnp.dot(aggregated, gcn_weight, preferred_element_type=jnp.float32)
    hidden = (features.astype(jnp.float32) + jax.nn.silu(preact)).astype(jnp.bfloat16)
    targets, fillers = slot_table(routes, expert_count, capacity)
    cotangent = (
        (route_weight[:, :, None] * out_grad[:, None, :].astype(jnp.float32))
        .astype(jnp.bfloat16)
        .reshape(-1, width)
    )
    present = (fillers > 0)[:, None]
    source_pair = jnp.maximum(fillers - 1, 0)
    nothing = jnp.zeros((), jnp.bfloat16)
    slot_shape = (dom_count, expert_local * capacity, width)
    send_hidden = jnp.where(present, hidden[source_pair // top_count], nothing).reshape(slot_shape)
    send_cot = jnp.where(present, cotangent[source_pair], nothing).reshape(slot_shape)
    mine_cot = lax.all_to_all(send_cot, "dom", split_axis=0, concat_axis=0, tiled=True)
    token_cot = lax.all_gather(mine_cot[None], "group", axis=0, tiled=True)
    mine_hidden = lax.all_to_all(send_hidden, "dom", split_axis=0, concat_axis=0, tiled=True)
    token_hidden = lax.all_gather(mine_hidden[None], "group", axis=0, tiled=True)
    sender_count = group_count * dom_count
    token_hidden = token_hidden.reshape(sender_count, expert_local, capacity, width)
    token_cot = token_cot.reshape(sender_count, expert_local, capacity, width)
    up_proj = jnp.einsum(
        "secd,edf->secf", token_hidden, up_weight, preferred_element_type=jnp.float32
    )
    active = jax.nn.silu(up_proj).astype(jnp.bfloat16)
    merged = lax.psum_scatter(
        jnp.einsum(
            "secf,efd->secd", active, down_weight, preferred_element_type=jnp.float32
        ).astype(jnp.bfloat16),
        "group",
        scatter_dimension=0,
        tiled=True,
    )
    expert_out = merged.reshape(dom_count, expert_local * capacity, width)
    returned = lax.all_to_all(expert_out, "dom", split_axis=0, concat_axis=0, tiled=True).reshape(
        expert_count * capacity, width
    )
    gathered = returned[targets].reshape(node_count, top_count, width)
    node_out = (
        hidden.astype(jnp.float32)
        + jnp.sum(route_weight[:, :, None] * gathered.astype(jnp.float32), axis=1)
    ).astype(jnp.bfloat16)
    grad_act = jnp.einsum(
        "secd,efd->secf", token_cot, down_weight, preferred_element_type=jnp.float32
    )
    grad_pre = (grad_act * silu_slope(up_proj)).astype(jnp.bfloat16)
    down_grad = jnp.einsum(
        "secf,secd->efd", active, token_cot, preferred_element_type=jnp.float32
    ).astype(jnp.bfloat16)
    up_grad = jnp.einsum(
        "secd,secf->edf", token_hidden, grad_pre, preferred_element_type=jnp.float32
    ).astype(jnp.bfloat16)
    return (node_out, up_grad, down_grad)


def solution(mesh):
    in_specs = (
        P(("dom", "group"), None),
        P(("dom", "group"), None),
        P(),
        P(("dom", "group"), None),
        P(("dom", "group"), None, None, None),
        P("dom", "group", None, None),
        P(("dom", "group"), None),
        P(("dom", "group"), None),
        P("dom", None, "group"),
        P("dom", "group", None),
    )
    out_specs = (P(("dom", "group"), None), P("dom", None, "group"), P("dom", "group", None))
    return jax.shard_map(local, mesh=mesh, in_specs=in_specs, out_specs=out_specs, check_vma=False)
```

profile of v0, /device:TPU:0, one launch (start us, length us, event | category | flops | bytes accessed | tf_op | source)
XLA Modules:
  0.0 192.9 jit_solution(4663778561806008242)
XLA Ops:
  7.2 0.0 copy-start
  7.2 0.0 copy-start.1
  7.2 0.0 copy-start.7
  7.2 0.9 reshape.153
  8.2 3.3 %gather_fusion = bf16[256,1024]{1,0:T(8,128)(2,1)} fusion(bf16[128,1024]{1,0:T(8,128)(2,1)} %param.10, s32[1024]{0:T(1024)S(1)} %pad_clamp_fusion.4), kind=kCustom, calls=%fused_computation | custom fusion | bytes 1049600 | tf_op jit(solution)/shard_map/gather | solution.py:51
  11.5 7.3 %all-to-all-start = ((bf16[8,32,1024]{2,1,0:T(8,128)(2,1)}), bf16[8,32,1024]{2,1,0:T(8,128)(2,1)}, u32[]{:S(2)}, u32[]{:S(2)}) async-start(bf16[8,32,1024]{2,1,0:T(8,128)(2,1)} %bitcast.1), calls=%async_computation | async-start | bytes 1048576 | tf_op jit(solution)/shard_map/all_to_all | solution.py:52
  18.8 0.0 all-gather.5.cloned.1.call-start
  18.8 0.1 copy.62
  19.0 0.1 eq.25
  19.1 0.1 eq.29
  19.3 0.1 copy.61
  19.4 0.1 mul.66
  19.5 0.6 reduce-window.6
  20.1 0.2 slice_reduce_fusion
  20.3 0.1 fusion.32
  20.4 1.4 scatter_custom_fusion
  21.9 0.0 copy-done.1
  21.9 0.8 copy.56
  22.7 1.2 mul.72
  24.0 1.7 mul.73
  25.7 0.1 copy.60
  25.8 0.1 mul.70
  25.9 0.1 broadcast_in_dim.43
  26.0 1.1 reduce_sum.29
  27.1 1.3 multiply_convert_fusion
  28.4 0.0 copy-start.6
  28.4 2.6 %gather_fusion.4 = bf16[320,1024]{1,0:T(8,128)(2,1)} fusion(bf16[256,1024]{1,0:T(8,128)(2,1)S(1)} %multiply_convert_fusion, s32[1024]{0:T(1024)S(1)} %get-tuple-element.16), kind=kCustom, calls=%fused_computation.4 | custom fusion | bytes 1312000 | tf_op jit(solution)/shard_map/gather | solution.py:78
  31.1 2.3 %all-to-all-done = bf16[8,32,1024]{2,1,0:T(8,128)(2,1)} async-done(((bf16[8,32,1024]{2,1,0:T(8,128)(2,1)}), bf16[8,32,1024]{2,1,0:T(8,128)(2,1)}, u32[]{:S(2)}, u32[]{:S(2)}) %all-to-all-start) | async-done | bytes 524320 | tf_op jit(solution)/shard_map/all_to_all | solution.py:52
  33.4 1.1 pad_maximum_fusion
  34.5 1.6 gather_fusion.1
  36.1 2.9 %fusion.24 = bf16[128,1024]{0,1:T(8,128)(2,1)S(1)} fusion(bf16[128,1024]{0,1:T(8,128)(2,1)} %copy.56, bf16[1024,1024]{1,0:T(8,128)(2,1)S(1)} %copy-done, bf16[4,128,1024]{2,1,0:T(8,128)(2,1)} %gather_fusion.1, f32[128]{0:T(128)S(1)} %add_sqrt_fusion, s32[1,4,128,128]{3,2,1,0:T(8,128)S(1)} %copy-done.6), kind=kOutput, calls=%fused_computation.38 | convolution fusion | flops 404160512 | bytes 3932672 | tf_op jit(solution)/shard_map/dot_general | solution.py:65
  38.9 0.0 copy-start.4
  38.9 0.0 copy-start.3
  39.0 0.1 copy.65
  39.1 2.6 %gather_fusion.2 = bf16[320,1024]{1,0:T(8,128)(2,1)} fusion(bf16[128,1024]{1,0:T(8,128)(2,1)S(1)} %copy.65, s32[1024]{0:T(1024)S(1)} %get-tuple-element.17), kind=kCustom, calls=%fused_computation.2 | custom fusion | bytes 1312000 | tf_op jit(solution)/shard_map/gather | solution.py:77
  41.8 1.2 broadcast_select_fusion
  43.0 21.4 %all_to_all.20 = bf16[8,40,1024]{2,1,0:T(8,128)(2,1)} all-to-all(bf16[8,40,1024]{2,1,0:T(8,128)(2,1)S(1)} %get-tuple-element.15), channel_id=1, replica_groups=mesh['dom'=8,'group'=4] {'dom'}, dimensions={0} | all-to-all | bytes 1310720 | tf_op jit(solution)/shard_map/all_to_all | solution.py:81
  64.4 0.0 all-gather.5.cloned.1.call-update
  64.4 0.0 all-gather.7.cloned.1.call-start
  64.5 20.7 %all_to_all.21 = bf16[8,40,1024]{2,1,0:T(8,128)(2,1)} all-to-all(bf16[8,40,1024]{2,1,0:T(8,128)(2,1)S(1)} %get-tuple-element.14), channel_id=1, replica_groups=mesh['dom'=8,'group'=4] {'dom'}, dimensions={0} | all-to-all | bytes 1310720 | tf_op jit(solution)/shard_map/all_to_all | solution.py:79
  85.2 0.0 all-gather.7.cloned.1.call-update
  85.2 0.2 reduce-scatter.4.cloned.1.call-start
  85.4 3.4 %all-gather.5.cloned.1.call-done = bf16[32,40,1024]{2,1,0:T(8,128)(2,1)} async-done(((bf16[8,40,1024]{2,1,0:T(8,128)(2,1)}), bf16[32,40,1024]{2,1,0:T(8,128)(2,1)}) %all-gather.5.cloned.1.call-update) | async-done | bytes 2621456 | tf_op jit(solution)/shard_map/all_gather | solution.py:82
  88.8 3.3 %copy.66 = bf16[32,40,1024]{2,0,1:T(8,128)(2,1)S(1)} copy(bf16[32,40,1024]{2,1,0:T(8,128)(2,1)} %all-gather.5.cloned.1.call-done) | data formatting | bytes 5242880 | tf_op jit(solution)/shard_map/all_gather | solution.py:82
  92.2 1.5 copy-done.2
  93.7 2.9 %fusion.7 = f32[2,32,20,1024]{3,1,2,0:T(8,128)S(1)} fusion(bf16[32,2,20,1024]{3,0,2,1:T(8,128)(2,1)S(1)} %bitcast.122, bf16[2,1024,1024]{2,1,0:T(8,128)(2,1)S(1)} %copy-done.9), kind=kOutput, calls=%fused_computation.19 | convolution fusion | flops 2684354560 | bytes 12058624 | tf_op jit(solution)/shard_map/secd,edf->secf/dot_general | solution.py:86
  96.6 3.1 %convert_bitcast_fusion = bf16[32,2,20,1024]{3,0,2,1:T(8,128)(2,1)S(1)} fusion(bf16[2,1024,1024]{2,1,0:T(8,128)(2,1)S(1)} %copy-done.10, f32[2,32,20,1024]{3,1,2,0:T(8,128)S(1)} %fusion.7), kind=kOutput, calls=%fused_computation.25 | convolution fusion | flops 2692218880 | bytes 12058624 | tf_op jit(solution)/shard_map/secf,efd->secd/dot_general | solution.py:91
  99.8 3.1 %copy.78 = bf16[32,2,20,1024]{3,2,1,0:T(8,128)(2,1)} copy(bf16[32,2,20,1024]{3,0,2,1:T(8,128)(2,1)S(1)} %convert_bitcast_fusion) | data formatting | bytes 5242880
  102.9 4.9 %reshape.226 = bf16[32,40960]{1,0:T(8,128)(2,1)} reshape(bf16[32,2,20,1024]{3,2,1,0:T(8,128)(2,1)} %copy.78) | data formatting | bytes 5242880
  107.8 0.0 reduce-scatter.4.cloned.1.call-update
  107.9 8.1 %all-gather.7.cloned.1.call-done = bf16[32,40,1024]{2,1,0:T(8,128)(2,1)} async-done(((bf16[8,40,1024]{2,1,0:T(8,128)(2,1)}), bf16[32,40,1024]{2,1,0:T(8,128)(2,1)}) %all-gather.7.cloned.1.call-update) | async-done | bytes 2621456 | tf_op jit(solution)/shard_map/all_gather | solution.py:80
  116.0 4.7 %copy.70 = bf16[32,40,1024]{2,0,1:T(8,128)(2,1)} copy(bf16[32,40,1024]{2,1,0:T(8,128)(2,1)} %all-gather.7.cloned.1.call-done) | data formatting | bytes 5242880 | tf_op jit(solution)/shard_map/all_gather | solution.py:80
  120.7 12.2 %bitcast_convert_fusion.1 = bf16[2,1024,1024]{2,1,0:T(8,128)(2,1)} fusion(bf16[32,2,20,1024]{3,0,2,1:T(8,128)(2,1)} %bitcast.123, f32[2,32,20,1024]{3,1,2,0:T(8,128)} %copy-done.12, bf16[32,2,20,1024]{3,0,2,1:T(8,128)(2,1)} %bitcast.124, bf16[2,1024,1024]{2,1,0:T(8,128)(2,1)} %param.19), kind=kOutput, calls=%fused_computation.7 | convolution fusion | flops 5382602752 | bytes 18874368 | tf_op jit(solution)/shard_map/secd,secf->edf/dot_general | solution.py:114
  132.9 20.3 %reduce-scatter.4.cloned.1.call-done = bf16[8,40960]{1,0:T(8,128)(2,1)} async-done(((bf16[32,40960]{1,0:T(8,128)(2,1)}), bf16[8,40960]{1,0:T(8,128)(2,1)}) %reduce-scatter.4.cloned.1.call-update) | async-done | bytes 655376
  153.2 2.3 %copy.67 = bf16[8,40,1024]{2,1,0:T(8,128)(2,1)} copy(bf16[8,40,1024]{2,0,1:T(8,128)(2,1)} %bitcast.128) | data formatting | bytes 1310720 | tf_op jit(solution)/shard_map/reshape | solution.py:98
  155.6 5.5 %all-to-all-start.2 = ((bf16[8,40,1024]{2,1,0:T(8,128)(2,1)}), bf16[8,40,1024]{2,1,0:T(8,128)(2,1)S(1)}, u32[]{:S(2)}, u32[]{:S(2)}) async-start(bf16[8,40,1024]{2,1,0:T(8,128)(2,1)} %copy.67), calls=%async_computation.2 | async-start | bytes 1310720 | tf_op jit(solution)/shard_map/all_to_all | solution.py:99
  161.1 8.9 %bitcast_convert_fusion = bf16[2,1024,1024]{2,1,0:T(8,128)(2,1)} fusion(bf16[32,2,20,1024]{3,0,2,1:T(8,128)(2,1)} %bitcast.125, f32[2,32,20,1024]{3,1,2,0:T(8,128)} %copy-done.12), kind=kOutput, calls=%fused_computation.6 | convolution fusion | flops 2693005312 | bytes 12058624 | tf_op jit(solution)/shard_map/secf,secd->efd/dot_general | solution.py:111
  169.9 8.4 %all-to-all-done.2 = bf16[8,40,1024]{2,1,0:T(8,128)(2,1)S(1)} async-done(((bf16[8,40,1024]{2,1,0:T(8,128)(2,1)}), bf16[8,40,1024]{2,1,0:T(8,128)(2,1)S(1)}, u32[]{:S(2)}, u32[]{:S(2)}) %all-to-all-start.2) | async-done | bytes 655392 | tf_op jit(solution)/shard_map/all_to_all | solution.py:99
  178.4 2.0 %gather_fusion.3 = bf16[256,1024]{1,0:T(8,128)(2,1)} fusion(bf16[320,1024]{1,0:T(8,128)(2,1)S(1)} %bitcast.120, s32[1024]{0:T(1024)S(1)} %pad_clamp_fusion.1), kind=kCustom, calls=%fused_computation.3 | custom fusion | bytes 1049600 | tf_op jit(solution)/shard_map/gather | solution.py:102
  180.3 1.7 reshape.164
  182.0 2.1 %multiply_reduce_fusion = f32[128,1024]{1,0:T(8,128)} fusion(f32[128,2,1024]{2,1,0:T(2,128)S(1)} %reshape.164, f32[128,2]{1,0:T(8,128)S(1)} %copy.60), kind=kLoop, calls=%fused_computation.32 | loop fusion | flops 393216 | bytes 1573888 | tf_op jit(solution)/shard_map/reduce_sum | solution.py:105
  184.2 1.2 copy.68
  185.4 0.1 add_convert_fusion
  185.5 0.9 copy.71
  (33 shorter events, 0.2 us)
Async XLA Ops:
  7.2 28.9 %copy-start = (bf16[1024,1024]{1,0:T(8,128)(2,1)S(1)}, bf16[1024,1024]{1,0:T(8,128)(2,1)}, u32[]{:S(2)}) copy-start(bf16[1024,1024]{1,0:T(8,128)(2,1)} %param.12) | copy-start | bytes 6291460
  7.2 14.7 %copy-start.1 = (bf16[128,1024]{1,0:T(8,128)(2,1)S(1)}, bf16[128,1024]{1,0:T(8,128)(2,1)}, u32[]{:S(2)}) copy-start(bf16[128,1024]{1,0:T(8,128)(2,1)} %param.10) | copy-start | bytes 786436
  7.2 11.6 %copy-start.7 = (s32[128,2]{0,1:T(2,128)S(1)}, s32[128,2]{0,1:T(2,128)}, u32[]{:S(2)}) copy-start(s32[128,2]{0,1:T(2,128)} %param.16) | copy-start | bytes 3076
  8.1 17.5 %copy-start.8 = (f32[128,2]{0,1:T(2,128)S(1)}, f32[128,2]{0,1:T(2,128)}, u32[]{:S(2)}) copy-start(f32[128,2]{0,1:T(2,128)} %param.17) | copy-start | bytes 3076
  11.5 21.9 %all-to-all-start = ((bf16[8,32,1024]{2,1,0:T(8,128)(2,1)}), bf16[8,32,1024]{2,1,0:T(8,128)(2,1)}, u32[]{:S(2)}, u32[]{:S(2)}) async-start(bf16[8,32,1024]{2,1,0:T(8,128)(2,1)} %bitcast.1), calls=%async_computation | async-start | bytes 1048576 | tf_op jit(solution)/shard_map/all_to_all | solution.py:52
  18.8 70.0 %all-gather.5.cloned.1.call-start = ((), (), s32[]{:S(2)}) async-start(), calls=%async_computation.5 | async-start | bytes 3276800 | tf_op jit(solution)/shard_map/all_gather | solution.py:82
  25.6 5.4 %copy-start.11 = (s32[1,4]{1,0:T(1,128)S(1)}, s32[1,4]{1,0:T(1,128)}, u32[]{:S(2)}) copy-start(s32[1,4]{1,0:T(1,128)} %param.13) | copy-start | bytes 52
  28.4 7.6 %copy-start.6 = (s32[1,4,128,128]{3,2,1,0:T(8,128)S(1)}, s32[1,4,128,128]{3,2,1,0:T(8,128)}, u32[]{:S(2)}) copy-start(s32[1,4,128,128]{3,2,1,0:T(8,128)} %param.14) | copy-start | bytes 786436
  38.9 2.8 %copy-start.4 = (bf16[128,1024]{0,1:T(8,128)(2,1)}, bf16[128,1024]{0,1:T(8,128)(2,1)S(1)}, u32[]{:S(2)}) copy-start(bf16[128,1024]{0,1:T(8,128)(2,1)S(1)} %fusion.24) | copy-start | bytes 786436
  38.9 2.8 %copy-start.3 = (bf16[320,1024]{1,0:T(8,128)(2,1)S(1)}, bf16[320,1024]{1,0:T(8,128)(2,1)}, u32[]{:S(2)}) copy-start(bf16[320,1024]{1,0:T(8,128)(2,1)} %gather_fusion.4) | copy-start | bytes 1966084
  64.4 51.5 %all-gather.7.cloned.1.call-start = ((), (), s32[]{:S(2)}) async-start(), calls=%async_computation.6 | async-start | bytes 3276800 | tf_op jit(solution)/shard_map/all_gather | solution.py:80
  85.2 68.0 %reduce-scatter.4.cloned.1.call-start = ((), (), s32[]{:S(2)}) async-start(), calls=%async_computation.7 | async-start | bytes 3276800
  88.8 4.9 %copy-start.9 = (bf16[2,1024,1024]{2,1,0:T(8,128)(2,1)S(1)}, bf16[2,1024,1024]{2,1,0:T(8,128)(2,1)}, u32[]{:S(2)}) copy-start(bf16[2,1024,1024]{2,1,0:T(8,128)(2,1)} %param.18) | copy-start | bytes 12582916
  92.1 1.5 copy-start.2
  93.7 2.9 %copy-start.10 = (bf16[2,1024,1024]{2,1,0:T(8,128)(2,1)S(1)}, bf16[2,1024,1024]{2,1,0:T(8,128)(2,1)}, u32[]{:S(2)}) copy-start(bf16[2,1024,1024]{2,1,0:T(8,128)(2,1)} %param.19) | copy-start | bytes 12582916
  96.6 3.2 %copy-start.12 = (f32[2,32,20,1024]{3,1,2,0:T(8,128)}, f32[2,32,20,1024]{3,1,2,0:T(8,128)S(1)}, u32[]{:S(2)}) copy-start(f32[2,32,20,1024]{3,1,2,0:T(8,128)S(1)} %fusion.7) | copy-start | bytes 15728644
  155.6 22.8 %all-to-all-start.2 = ((bf16[8,40,1024]{2,1,0:T(8,128)(2,1)}), bf16[8,40,1024]{2,1,0:T(8,128)(2,1)S(1)}, u32[]{:S(2)}, u32[]{:S(2)}) async-start(bf16[8,40,1024]{2,1,0:T(8,128)(2,1)} %copy.67), calls=%async_computation.2 | async-start | bytes 1310720 | tf_op jit(solution)/shard_map/all_to_all | solution.py:99
  178.4 7.0 %copy-start.5 = (bf16[128,1024]{0,1:T(8,128)(2,1)S(1)}, bf16[128,1024]{0,1:T(8,128)(2,1)}, u32[]{:S(2)}) copy-start(bf16[128,1024]{0,1:T(8,128)(2,1)} %copy-done.4) | copy-start | bytes 786436
Sparse Core Ops, SparseCore 0:
  64.5 24.2 all-gather.4
  90.4 25.5 all-gather.6
  118.5 34.6 reduce-scatter.3
where the time goes:
time: 194 us; the launch traced here: 193 us
  local copies, waits for them, and re-layouts  43.4 us (22%)
  waiting for transfers between devices  42.6 us (22%)
  blocking collectives  42.1 us (22%)
  matrix products  30 us (15%)
  between operations  14 us (7%)
  starting transfers between devices  13.1 us (7%)
  other arithmetic  7.74 us (4%)
    all_to_all x1, blocking collectives, local(): lax.all_to_all(send_hidden, 'dom', split_axis=0, concat_axis=0, tiled=True)  21.4 us
    all_to_all x1, blocking collectives, local(): lax.all_to_all(send_cot, 'dom', split_axis=0, concat_axis=0, tiled=True)  20.7 us
    unnamed x4, waiting for transfers between devices  20.4 us
    dot_general x1, matrix products, local(): jnp.einsum('secd,secf->edf', token_hidden, grad_pre, preferred_element_ty...  12.2 us
    unnamed x32, local copies, waits for them, and re-layouts  11.6 us
    dot_general x1, matrix products, local(): jnp.einsum('secf,secd->efd', active, token_cot, preferred_element_type=jn...  8.86 us
    all_to_all x1, waiting for transfers between devices, local(): lax.all_to_all(expert_out, 'dom', split_axis=0, concat_axis=0, tiled=True)  8.44 us
    all_gather x1, waiting for transfers between devices, local(): token_cot = lax.all_gather(mine_cot[None], 'group', axis=0, tiled=True)  8.1 us
  transfers between devices with their start and end apart: 5, of which 5 were waited for; matrix products, arithmetic and copies ran while one was open for 29% of the time, Pallas kernels for 0%

commit v1 on v0

--- a/solution.py
+++ b/solution.py
@@ -2,6 +2,17 @@
 import jax.numpy as jnp
 from jax import lax
 from jax.sharding import PartitionSpec as P
+
+
+def cut_along(value, dim, length):
+    before, after = (value.shape[:dim], value.shape[dim + 1 :])
+    return jnp.moveaxis(value.reshape(*before, length, -1, *after), dim, 0)
+
+
+def joined_along(blocks, dim):
+    blocks = jnp.moveaxis(blocks, 0, dim)
+    shape = blocks.shape
+    return blocks.reshape(*shape[:dim], shape[dim] * shape[dim + 1], *shape[dim + 2 :])
 
 
 def silu_slope(values):
@@ -78,7 +89,14 @@
     send_cot = jnp.where(present, cotangent[source_pair], nothing).reshape(slot_shape)
     mine_cot = lax.all_to_all(send_cot, "dom", split_axis=0, concat_axis=0, tiled=True)
     token_cot = lax.all_gather(mine_cot[None], "group", axis=0, tiled=True)
-    mine_hidden = lax.all_to_all(send_hidden, "dom", split_axis=0, concat_axis=0, tiled=True)
+    size, mine = (lax.axis_size("dom"), lax.axis_index("dom"))
+    blocks = cut_along(send_hidden, 0, size)
+    gathered_2 = [blocks[mine]]
+    for turn in range(1, size):
+        sent = blocks[mine ^ turn]
+        gathered_2.append(lax.ppermute(sent, "dom", [(i, i ^ turn) for i in range(size)]))
+    blocks = jnp.stack(gathered_2)[mine ^ jnp.arange(size)]
+    mine_hidden = joined_along(blocks, 0)
     token_hidden = lax.all_gather(mine_hidden[None], "group", axis=0, tiled=True)
     sender_count = group_count * dom_count
     token_hidden = token_hidden.reshape(sender_count, expert_local, capacity, width)

time: 194 us -> 196 us (1.010)
  blocking collectives: 42.1 us -> 21.8 us
  starting transfers between devices: 13.1 us -> 24.4 us
  waiting for transfers between devices: 42.6 us -> 52.6 us
    all_to_all x1 -> x0, blocking collectives: 21.4 us -> none  [local(): lax.all_to_all(send_hidden, 'dom', split_axis=0, concat_axis=0, tiled=True)]
    ppermute x0 -> x7, starting transfers between devices: none -> 11.3 us  [local(): lax.ppermute(sent, 'dom', [(i, i ^ turn) for i in range(size)])]
    all_to_all x1, waiting for transfers between devices: 2.26 us -> 11.9 us  [local(): lax.all_to_all(outgoing, 'dom', split_axis=0, concat_axis=0, tiled=True)]
    ppermute x0 -> x7, waiting for transfers between devices: none -> 6.9 us  [local(): lax.ppermute(sent, 'dom', [(i, i ^ turn) for i in range(size)])]
    all_gather x1, waiting for transfers between devices: 3.38 us -> 0.02 us  [local(): lax.all_gather(mine_hidden[None], 'group', axis=0, tiled=True)]
    all_gather x1, waiting for transfers between devices: 8.1 us -> 5.07 us  [local(): token_cot = lax.all_gather(mine_cot[None], 'group', axis=0, tiled=True)]
    unnamed x32 -> x36, local copies, waits for them, and re-layouts: 11.6 us -> 13.1 us
  transfers between devices with their start and end apart: 5 -> 12, of which waited for: 5 -> 6; matrix products, arithmetic and copies ran while one was open for 29% -> 27% of each run, Pallas kernels for 0% -> 0%
where the time goes in v1:
time: 196 us; the launch traced here: 195 us
  waiting for transfers between devices  52.6 us (27%)
  local copies, waits for them, and re-layouts  45.1 us (23%)
  matrix products  30.1 us (15%)
  starting transfers between devices  24.4 us (12%)
  blocking collectives  21.8 us (11%)
  between operations  14.2 us (7%)
  other arithmetic  6.63 us (3%)
    all_to_all x1, blocking collectives, local(): lax.all_to_all(send_cot, 'dom', split_axis=0, concat_axis=0, tiled=True)  21.8 us
    unnamed x4, waiting for transfers between devices  20.4 us
    unnamed x36, local copies, waits for them, and re-layouts  13.1 us
    dot_general x1, matrix products, local(): jnp.einsum('secd,secf->edf', token_hidden, grad_pre, preferred_element_ty...  12.2 us
    all_to_all x1, waiting for transfers between devices, local(): lax.all_to_all(outgoing, 'dom', split_axis=0, concat_axis=0, tiled=True)  11.9 us
    ppermute x7, starting transfers between devices, local(): lax.ppermute(sent, 'dom', [(i, i ^ turn) for i in range(size)])  11.3 us
    dot_general x1, matrix products, local(): jnp.einsum('secf,secd->efd', active, token_cot, preferred_element_type=jn...  8.86 us
    all_to_all x1, waiting for transfers between devices, local(): lax.all_to_all(expert_out, 'dom', split_axis=0, concat_axis=0, tiled=True)  8.44 us
  transfers between devices with their start and end apart: 12, of which 6 were waited for; matrix products, arithmetic and copies ran while one was open for 27% of the time, Pallas kernels for 0%

profile of v1, /device:TPU:0, one launch (start us, length us, event | category | flops | bytes accessed | tf_op | source)
XLA Modules:
  0.0 194.8 jit_solution(8032662026414236810)
XLA Ops:
  7.2 0.8 broadcast_multiply_fusion
  8.0 0.8 copy.62
  8.8 0.1 eq.25
  9.0 0.1 eq.29
  9.1 0.1 copy.61
  9.2 0.1 mul.66
  9.4 0.6 reduce-window.6
  10.0 0.2 slice_reduce_fusion
  10.2 0.8 reshape.179
  11.0 0.1 fusion.32
  11.1 3.3 %gather_fusion = bf16[256,1024]{1,0:T(8,128)(2,1)} fusion(bf16[128,1024]{1,0:T(8,128)(2,1)} %param.10, s32[1024]{0:T(1024)S(1)} %pad_clamp_fusion.5), kind=kCustom, calls=%fused_computation | custom fusion | bytes 1049600 | tf_op jit(solution)/shard_map/gather | solution.py:62
  14.4 7.3 %all-to-all-start = ((bf16[8,32,1024]{2,1,0:T(8,128)(2,1)}), bf16[8,32,1024]{2,1,0:T(8,128)(2,1)S(1)}, u32[]{:S(2)}, u32[]{:S(2)}) async-start(bf16[8,32,1024]{2,1,0:T(8,128)(2,1)} %bitcast.1), calls=%async_computation | async-start | bytes 1048576 | tf_op jit(solution)/shard_map/all_to_all | solution.py:63
  21.8 1.4 scatter_custom_fusion
  23.2 0.8 copy.56
  24.0 0.1 reduce_sum.29
  24.2 0.1 broadcast_in_dim.45
  24.3 11.9 %all-to-all-done = bf16[8,32,1024]{2,1,0:T(8,128)(2,1)S(1)} async-done(((bf16[8,32,1024]{2,1,0:T(8,128)(2,1)}), bf16[8,32,1024]{2,1,0:T(8,128)(2,1)S(1)}, u32[]{:S(2)}, u32[]{:S(2)}) %all-to-all-start) | async-done | bytes 524320 | tf_op jit(solution)/shard_map/all_to_all | solution.py:63
  36.2 0.8 copy-done.3
  37.0 1.1 pad_maximum_fusion
  38.1 1.6 gather_fusion.1
  39.7 3.0 %fusion.24 = bf16[128,1024]{0,1:T(8,128)(2,1)S(1)} fusion(bf16[128,1024]{0,1:T(8,128)(2,1)} %copy.56, bf16[1024,1024]{1,0:T(8,128)(2,1)S(1)} %copy-done, bf16[4,128,1024]{2,1,0:T(8,128)(2,1)} %gather_fusion.1, f32[128]{0:T(128)S(1)} %add_sqrt_fusion, s32[1,4,128,128]{3,2,1,0:T(8,128)} %param.14), kind=kOutput, calls=%fused_computation.39 | convolution fusion | flops 404160512 | bytes 3932672 | tf_op jit(solution)/shard_map/dot_general | solution.py:76
  42.6 0.1 copy.65
  42.8 2.1 %gather_fusion.2 = bf16[320,1024]{1,0:T(8,128)(2,1)S(1)} fusion(bf16[128,1024]{1,0:T(8,128)(2,1)S(1)} %copy.65, s32[1024]{0:T(1024)S(1)} %pad_clamp_fusion.3), kind=kCustom, calls=%fused_computation.2 | custom fusion | bytes 1312000 | tf_op jit(solution)/shard_map/gather | solution.py:88
  44.9 0.1 broadcast_select_fusion.1
  45.0 0.1 dynamic-slice_bitcast_fusion
  45.1 1.5 collective-permute-start
  46.6 2.0 %collective-permute-start.2 = (bf16[1,40,1024]{2,1,0:T(8,128)(2,1)S(1)}, bf16[1,40,1024]{2,1,0:T(8,128)(2,1)S(1)}, u32[]{:S(2)}, u32[]{:S(2)}) collective-permute-start(bf16[1,40,1024]{2,1,0:T(8,128)(2,1)S(1)} %get-tuple-element.16), channel_id=1, source_target_pairs={{0,12},{4,8},{8,4},{12,0},{16,28},{20,24},{24,20},{28,16},{1,13},{... | collective-permute-start | bytes 245768 | tf_op jit(solution)/shard_map/ppermute | solution.py:97
  48.6 0.1 collective-permute-start.3
  48.8 3.7 %collective-permute-start.4 = (bf16[1,40,1024]{2,1,0:T(8,128)(2,1)S(1)}, bf16[1,40,1024]{2,1,0:T(8,128)(2,1)S(1)}, u32[]{:S(2)}, u32[]{:S(2)}) collective-permute-start(bf16[1,40,1024]{2,1,0:T(8,128)(2,1)S(1)} %get-tuple-element.14), channel_id=1, source_target_pairs={{0,20},{4,16},{8,28},{12,24},{16,4},{20,0},{24,12},{28,8},{1,21},{... | collective-permute-start | bytes 245768 | tf_op jit(solution)/shard_map/ppermute | solution.py:97
  52.5 1.5 collective-permute-start.5
  53.9 2.4 %collective-permute-start.6 = (bf16[1,40,1024]{2,1,0:T(8,128)(2,1)S(1)}, bf16[1,40,1024]{2,1,0:T(8,128)(2,1)S(1)}, u32[]{:S(2)}, u32[]{:S(2)}) collective-permute-start(bf16[1,40,1024]{2,1,0:T(8,128)(2,1)S(1)} %get-tuple-element.12), channel_id=1, source_target_pairs={{0,28},{4,24},{8,20},{12,16},{16,12},{20,8},{24,4},{28,0},{1,29},{... | collective-permute-start | bytes 245768 | tf_op jit(solution)/shard_map/ppermute | solution.py:97
  56.4 4.6 %collective-permute-done.3 = bf16[1,40,1024]{2,1,0:T(8,128)(2,1)S(1)} collective-permute-done((bf16[1,40,1024]{2,1,0:T(8,128)(2,1)S(1)}, bf16[1,40,1024]{2,1,0:T(8,128)(2,1)S(1)}, u32[]{:S(2)}, u32[]{:S(2)}) %collective-permute-start.3) | collective-permute-done | bytes 81952 | tf_op jit(solution)/shard_map/ppermute | solution.py:97
  61.0 2.3 %collective-permute-done.4 = bf16[1,40,1024]{2,1,0:T(8,128)(2,1)S(1)} collective-permute-done((bf16[1,40,1024]{2,1,0:T(8,128)(2,1)S(1)}, bf16[1,40,1024]{2,1,0:T(8,128)(2,1)S(1)}, u32[]{:S(2)}, u32[]{:S(2)}) %collective-permute-start.4) | collective-permute-done | bytes 81952 | tf_op jit(solution)/shard_map/ppermute | solution.py:97
  63.3 1.4 gather_fusion.3
  64.8 0.0 all-gather.7.cloned.1.call-start
  64.9 0.1 copy.60
  65.0 1.2 mul.72
  66.2 1.7 mul.73
  67.9 0.1 mul.70
  68.1 1.4 multiply_convert_fusion
  69.4 2.1 %gather_fusion.5 = bf16[320,1024]{1,0:T(8,128)(2,1)S(1)} fusion(bf16[256,1024]{1,0:T(8,128)(2,1)S(1)} %multiply_convert_fusion, s32[1024]{0:T(1024)S(1)} %pad_clamp_fusion), kind=kCustom, calls=%fused_computation.5 | custom fusion | bytes 1312000 | tf_op jit(solution)/shard_map/gather | solution.py:89
  71.5 0.1 broadcast_select_fusion
  71.7 21.8 %all_to_all.15 = bf16[8,40,1024]{2,1,0:T(8,128)(2,1)} all-to-all(bf16[8,40,1024]{2,1,0:T(8,128)(2,1)S(1)} %broadcast_select_fusion), channel_id=1, replica_groups=mesh['dom'=8,'group'=4] {'dom'}, dimensions={0} | all-to-all | bytes 1310720 | tf_op jit(solution)/shard_map/all_to_all | solution.py:90
  93.5 0.2 reduce-scatter.4.cloned.1.call-start
  93.8 3.3 %copy.66 = bf16[32,40,1024]{2,0,1:T(8,128)(2,1)S(1)} copy(bf16[32,40,1024]{2,1,0:T(8,128)(2,1)} %all-gather.5.cloned.1.call-done) | data formatting | bytes 5242880 | tf_op jit(solution)/shard_map/all_gather | solution.py:100
  97.1 1.5 copy-done.2
  98.7 2.9 %fusion.7 = f32[2,32,20,1024]{3,1,2,0:T(8,128)S(1)} fusion(bf16[32,2,20,1024]{3,0,2,1:T(8,128)(2,1)S(1)} %bitcast.153, bf16[2,1024,1024]{2,1,0:T(8,128)(2,1)S(1)} %copy-done.8), kind=kOutput, calls=%fused_computation.20 | convolution fusion | flops 2684354560 | bytes 12058624 | tf_op jit(solution)/shard_map/secd,edf->secf/dot_general | solution.py:104
  101.6 3.1 %convert_bitcast_fusion = bf16[32,2,20,1024]{3,0,2,1:T(8,128)(2,1)S(1)} fusion(bf16[2,1024,1024]{2,1,0:T(8,128)(2,1)S(1)} %copy-done.9, f32[2,32,20,1024]{3,1,2,0:T(8,128)S(1)} %fusion.7), kind=kOutput, calls=%fused_computation.26 | convolution fusion | flops 2692218880 | bytes 12058624 | tf_op jit(solution)/shard_map/secf,efd->secd/dot_general | solution.py:109
  104.7 3.1 %copy.78 = bf16[32,2,20,1024]{3,2,1,0:T(8,128)(2,1)} copy(bf16[32,2,20,1024]{3,0,2,1:T(8,128)(2,1)S(1)} %convert_bitcast_fusion) | data formatting | bytes 5242880
  107.8 4.9 %reshape.262 = bf16[32,40960]{1,0:T(8,128)(2,1)} reshape(bf16[32,2,20,1024]{3,2,1,0:T(8,128)(2,1)} %copy.78) | data formatting | bytes 5242880
  112.8 5.1 %all-gather.7.cloned.1.call-done = bf16[32,40,1024]{2,1,0:T(8,128)(2,1)} async-done(((bf16[8,40,1024]{2,1,0:T(8,128)(2,1)}), bf16[32,40,1024]{2,1,0:T(8,128)(2,1)}) %all-gather.7.cloned.1.call-update) | async-done | bytes 2621456 | tf_op jit(solution)/shard_map/all_gather | solution.py:91
  117.9 4.7 %copy.70 = bf16[32,40,1024]{2,0,1:T(8,128)(2,1)} copy(bf16[32,40,1024]{2,1,0:T(8,128)(2,1)} %all-gather.7.cloned.1.call-done) | data formatting | bytes 5242880 | tf_op jit(solution)/shard_map/all_gather | solution.py:91
  122.6 12.2 %bitcast_convert_fusion.1 = bf16[2,1024,1024]{2,1,0:T(8,128)(2,1)} fusion(bf16[32,2,20,1024]{3,0,2,1:T(8,128)(2,1)} %bitcast.154, f32[2,32,20,1024]{3,1,2,0:T(8,128)} %copy-done.11, bf16[32,2,20,1024]{3,0,2,1:T(8,128)(2,1)} %bitcast.155, bf16[2,1024,1024]{2,1,0:T(8,128)(2,1)} %param.19), kind=kOutput, calls=%fused_computation.8 | convolution fusion | flops 5382602752 | bytes 18874368 | tf_op jit(solution)/shard_map/secd,secf->edf/dot_general | solution.py:132
  134.8 20.3 %reduce-scatter.4.cloned.1.call-done = bf16[8,40960]{1,0:T(8,128)(2,1)} async-done(((bf16[32,40960]{1,0:T(8,128)(2,1)}), bf16[8,40960]{1,0:T(8,128)(2,1)}) %reduce-scatter.4.cloned.1.call-update) | async-done | bytes 655376
  155.1 2.3 %copy.67 = bf16[8,40,1024]{2,1,0:T(8,128)(2,1)} copy(bf16[8,40,1024]{2,0,1:T(8,128)(2,1)} %bitcast.161) | data formatting | bytes 1310720 | tf_op jit(solution)/shard_map/reshape | solution.py:116
  157.4 5.5 %all-to-all-start.1 = ((bf16[8,40,1024]{2,1,0:T(8,128)(2,1)}), bf16[8,40,1024]{2,1,0:T(8,128)(2,1)S(1)}, u32[]{:S(2)}, u32[]{:S(2)}) async-start(bf16[8,40,1024]{2,1,0:T(8,128)(2,1)} %copy.67), calls=%async_computation.1 | async-start | bytes 1310720 | tf_op jit(solution)/shard_map/all_to_all | solution.py:117
  162.9 8.9 %bitcast_convert_fusion = bf16[2,1024,1024]{2,1,0:T(8,128)(2,1)} fusion(bf16[32,2,20,1024]{3,0,2,1:T(8,128)(2,1)} %bitcast.156, f32[2,32,20,1024]{3,1,2,0:T(8,128)} %copy-done.11), kind=kOutput, calls=%fused_computation.7 | convolution fusion | flops 2693005312 | bytes 12058624 | tf_op jit(solution)/shard_map/secf,secd->efd/dot_general | solution.py:129
  171.8 8.4 %all-to-all-done.1 = bf16[8,40,1024]{2,1,0:T(8,128)(2,1)S(1)} async-done(((bf16[8,40,1024]{2,1,0:T(8,128)(2,1)}), bf16[8,40,1024]{2,1,0:T(8,128)(2,1)S(1)}, u32[]{:S(2)}, u32[]{:S(2)}) %all-to-all-start.1) | async-done | bytes 655392 | tf_op jit(solution)/shard_map/all_to_all | solution.py:117
  180.2 2.0 %gather_fusion.4 = bf16[256,1024]{1,0:T(8,128)(2,1)} fusion(bf16[320,1024]{1,0:T(8,128)(2,1)S(1)} %bitcast.151, s32[1024]{0:T(1024)S(1)} %pad_clamp_fusion.1), kind=kCustom, calls=%fused_computation.4 | custom fusion | bytes 1049600 | tf_op jit(solution)/shard_map/gather | solution.py:120
  182.2 1.7 reshape.190
  183.9 2.2 %multiply_reduce_fusion = f32[128,1024]{1,0:T(8,128)} fusion(f32[128,2,1024]{2,1,0:T(2,128)S(1)} %reshape.190, f32[128,2]{1,0:T(8,128)S(1)} %copy-done.5), kind=kLoop, calls=%fused_computation.33 | loop fusion | flops 393216 | bytes 1573888 | tf_op jit(solution)/shard_map/reduce_sum | solution.py:123
  186.1 1.2 copy.68
  187.3 0.1 add_convert_fusion
  187.4 0.9 copy.71
  (56 shorter events, 0.4 us)
Async XLA Ops:
  7.2 32.5 %copy-start = (bf16[1024,1024]{1,0:T(8,128)(2,1)S(1)}, bf16[1024,1024]{1,0:T(8,128)(2,1)}, u32[]{:S(2)}) copy-start(bf16[1024,1024]{1,0:T(8,128)(2,1)} %param.12) | copy-start | bytes 6291460
  7.2 16.0 %copy-start.1 = (bf16[128,1024]{1,0:T(8,128)(2,1)S(1)}, bf16[128,1024]{1,0:T(8,128)(2,1)}, u32[]{:S(2)}) copy-start(bf16[128,1024]{1,0:T(8,128)(2,1)} %param.10) | copy-start | bytes 786436
  7.2 16.9 %copy-start.6 = (s32[1,4,128,128]{3,2,1,0:T(8,128)S(1)}, s32[1,4,128,128]{3,2,1,0:T(8,128)}, u32[]{:S(2)}) copy-start(s32[1,4,128,128]{3,2,1,0:T(8,128)} %param.14) | copy-start | bytes 786436
  7.2 17.0 %copy-start.10 = (s32[1,4]{1,0:T(1,128)S(1)}, s32[1,4]{1,0:T(1,128)}, u32[]{:S(2)}) copy-start(s32[1,4]{1,0:T(1,128)} %param.13) | copy-start | bytes 52
  14.4 21.8 %all-to-all-start = ((bf16[8,32,1024]{2,1,0:T(8,128)(2,1)}), bf16[8,32,1024]{2,1,0:T(8,128)(2,1)S(1)}, u32[]{:S(2)}, u32[]{:S(2)}) async-start(bf16[8,32,1024]{2,1,0:T(8,128)(2,1)} %bitcast.1), calls=%async_computation | async-start | bytes 1048576 | tf_op jit(solution)/shard_map/all_to_all | solution.py:63
  21.7 72.1 %all-gather.5.cloned.1.call-start = ((), (), s32[]{:S(2)}) async-start(), calls=%async_computation.4 | async-start | bytes 3276800 | tf_op jit(solution)/shard_map/all_gather | solution.py:100
  36.2 0.8 copy-start.3
  44.9 20.0 %copy-start.7 = (f32[128,2]{0,1:T(2,128)S(1)}, f32[128,2]{0,1:T(2,128)}, u32[]{:S(2)}) copy-start(f32[128,2]{0,1:T(2,128)} %param.17) | copy-start | bytes 3076
  45.1 7.4 %collective-permute-start = (bf16[1,40,1024]{2,1,0:T(8,128)(2,1)S(1)}, bf16[1,40,1024]{2,1,0:T(8,128)(2,1)S(1)}, u32[]{:S(2)}, u32[]{:S(2)}) collective-permute-start(bf16[1,40,1024]{2,1,0:T(8,128)(2,1)S(1)} %get-tuple-element.18), channel_id=1, source_target_pairs={{0,4},{4,0},{8,12},{12,8},{16,20},{20,16},{24,28},{28,24},{1,5},{5... | collective-permute-start | bytes 245768 | tf_op jit(solution)/shard_map/ppermute | solution.py:97
  46.6 7.3 %collective-permute-start.1 = (bf16[1,40,1024]{2,1,0:T(8,128)(2,1)S(1)}, bf16[1,40,1024]{2,1,0:T(8,128)(2,1)S(1)}, u32[]{:S(2)}, u32[]{:S(2)}) collective-permute-start(bf16[1,40,1024]{2,1,0:T(8,128)(2,1)S(1)} %get-tuple-element.17), channel_id=1, source_target_pairs={{0,8},{4,12},{8,0},{12,4},{16,24},{20,28},{24,16},{28,20},{1,9},{5... | collective-permute-start | bytes 245768 | tf_op jit(solution)/shard_map/ppermute | solution.py:97
  46.6 9.8 %collective-permute-start.2 = (bf16[1,40,1024]{2,1,0:T(8,128)(2,1)S(1)}, bf16[1,40,1024]{2,1,0:T(8,128)(2,1)S(1)}, u32[]{:S(2)}, u32[]{:S(2)}) collective-permute-start(bf16[1,40,1024]{2,1,0:T(8,128)(2,1)S(1)} %get-tuple-element.16), channel_id=1, source_target_pairs={{0,12},{4,8},{8,4},{12,0},{16,28},{20,24},{24,20},{28,16},{1,13},{... | collective-permute-start | bytes 245768 | tf_op jit(solution)/shard_map/ppermute | solution.py:97
  48.6 12.3 %collective-permute-start.3 = (bf16[1,40,1024]{2,1,0:T(8,128)(2,1)S(1)}, bf16[1,40,1024]{2,1,0:T(8,128)(2,1)S(1)}, u32[]{:S(2)}, u32[]{:S(2)}) collective-permute-start(bf16[1,40,1024]{2,1,0:T(8,128)(2,1)S(1)} %get-tuple-element.15), channel_id=1, source_target_pairs={{0,16},{4,20},{8,24},{12,28},{16,0},{20,4},{24,8},{28,12},{1,17},{... | collective-permute-start | bytes 245768 | tf_op jit(solution)/shard_map/ppermute | solution.py:97
  48.8 14.5 %collective-permute-start.4 = (bf16[1,40,1024]{2,1,0:T(8,128)(2,1)S(1)}, bf16[1,40,1024]{2,1,0:T(8,128)(2,1)S(1)}, u32[]{:S(2)}, u32[]{:S(2)}) collective-permute-start(bf16[1,40,1024]{2,1,0:T(8,128)(2,1)S(1)} %get-tuple-element.14), channel_id=1, source_target_pairs={{0,20},{4,16},{8,28},{12,24},{16,4},{20,0},{24,12},{28,8},{1,21},{... | collective-permute-start | bytes 245768 | tf_op jit(solution)/shard_map/ppermute | solution.py:97
  52.5 10.8 %collective-permute-start.5 = (bf16[1,40,1024]{2,1,0:T(8,128)(2,1)S(1)}, bf16[1,40,1024]{2,1,0:T(8,128)(2,1)S(1)}, u32[]{:S(2)}, u32[]{:S(2)}) collective-permute-start(bf16[1,40,1024]{2,1,0:T(8,128)(2,1)S(1)} %get-tuple-element.13), channel_id=1, source_target_pairs={{0,24},{4,28},{8,16},{12,20},{16,8},{20,12},{24,0},{28,4},{1,25},{... | collective-permute-start | bytes 245768 | tf_op jit(solution)/shard_map/ppermute | solution.py:97
  53.9 9.4 %collective-permute-start.6 = (bf16[1,40,1024]{2,1,0:T(8,128)(2,1)S(1)}, bf16[1,40,1024]{2,1,0:T(8,128)(2,1)S(1)}, u32[]{:S(2)}, u32[]{:S(2)}) collective-permute-start(bf16[1,40,1024]{2,1,0:T(8,128)(2,1)S(1)} %get-tuple-element.12), channel_id=1, source_target_pairs={{0,28},{4,24},{8,20},{12,16},{16,12},{20,8},{24,4},{28,0},{1,29},{... | collective-permute-start | bytes 245768 | tf_op jit(solution)/shard_map/ppermute | solution.py:97
  64.8 53.1 %all-gather.7.cloned.1.call-start = ((), (), s32[]{:S(2)}) async-start(), calls=%async_computation.5 | async-start | bytes 3276800 | tf_op jit(solution)/shard_map/all_gather | solution.py:91
  65.0 3.1 %copy-start.4 = (f32[128,2]{1,0:T(8,128)}, f32[128,2]{1,0:T(8,128)S(1)}, u32[]{:S(2)}) copy-start(f32[128,2]{1,0:T(8,128)S(1)} %copy.60) | copy-start | bytes 3076
  93.5 61.6 %reduce-scatter.4.cloned.1.call-start = ((), (), s32[]{:S(2)}) async-start(), calls=%async_computation.6 | async-start | bytes 3276800
  93.8 4.9 %copy-start.8 = (bf16[2,1024,1024]{2,1,0:T(8,128)(2,1)S(1)}, bf16[2,1024,1024]{2,1,0:T(8,128)(2,1)}, u32[]{:S(2)}) copy-start(bf16[2,1024,1024]{2,1,0:T(8,128)(2,1)} %param.18) | copy-start | bytes 12582916
  97.1 1.6 copy-start.2
  98.7 2.9 %copy-start.9 = (bf16[2,1024,1024]{2,1,0:T(8,128)(2,1)S(1)}, bf16[2,1024,1024]{2,1,0:T(8,128)(2,1)}, u32[]{:S(2)}) copy-start(bf16[2,1024,1024]{2,1,0:T(8,128)(2,1)} %param.19) | copy-start | bytes 12582916
  101.6 3.1 %copy-start.11 = (f32[2,32,20,1024]{3,1,2,0:T(8,128)}, f32[2,32,20,1024]{3,1,2,0:T(8,128)S(1)}, u32[]{:S(2)}) copy-start(f32[2,32,20,1024]{3,1,2,0:T(8,128)S(1)} %fusion.7) | copy-start | bytes 15728644
  157.4 22.8 %all-to-all-start.1 = ((bf16[8,40,1024]{2,1,0:T(8,128)(2,1)}), bf16[8,40,1024]{2,1,0:T(8,128)(2,1)S(1)}, u32[]{:S(2)}, u32[]{:S(2)}) async-start(bf16[8,40,1024]{2,1,0:T(8,128)(2,1)} %copy.67), calls=%async_computation.1 | async-start | bytes 1310720 | tf_op jit(solution)/shard_map/all_to_all | solution.py:117
  171.8 12.1 %copy-start.5 = (f32[128,2]{1,0:T(8,128)S(1)}, f32[128,2]{1,0:T(8,128)}, u32[]{:S(2)}) copy-start(f32[128,2]{1,0:T(8,128)} %copy-done.4) | copy-start | bytes 3076
Sparse Core Ops, SparseCore 0:
  64.9 25.7 all-gather.4
  93.6 24.1 all-gather.6
  120.4 34.6 reduce-scatter.3
